TPU v7x, 32 devices: a whole 2x2x4 slice. The times are simulated.
32 devices in a mesh: row: 4 (over x, core), col: 8 (over z, y).
Axes of the slice: x: 2, y: 2, z: 4, core: 2. Of those that a mesh axis runs over, the one named last changes fastest.
Arguments:
- vectors: float32 [16, 4096], P(None, ('row', 'col')), may hold values from -12 to 12, as said below
- diag_energy: float32 [4096], P(('row', 'col')), may hold values from 0.5 to 4
- blocks: float32 [4, 192, 128, 128], P('row', 'col'), may hold values from -0.078125 to 0.078125
- block_row: int32 [4, 192], P('row', 'col'), may hold values from 0 to 7
- block_col: int32 [4, 192], P('row', 'col'), may hold values from 0 to 3
Outputs:
- image: float32 [16, 4096], P(None, ('row', 'col'))
- resid: float32 [16, 4096], P(None, ('row', 'col'))
Inputs may be any that keep to these rules, and one draw needn't show every extreme that they name: `vectors`: each row of X holds independent entries; the Gram matrix X X^T is positive definite.
All inputs are finite; a program needn't handle non-finite values.
Results may differ from a plain program's by a relative error of at most 0.0003.
Values sent between devices are 32-bit elements; how exact they have to be, the bound alone decides.
A program may use at most 64 MiB of HBM per device.

v0:
```python
import jax
import jax.numpy as jnp
from jax import lax
from jax.sharding import PartitionSpec as P

BLK = 128


def solve_metric(metric, gram):
    highest = lax.Precision.HIGHEST
    order = metric.shape[0]
    index = jnp.arange(order)
    factor = jnp.zeros_like(metric)
    for column in range(order):
        onehot = (index == column).astype(jnp.float32)
        rest = metric[:, column] - jnp.dot(factor, factor[column, :], precision=highest)
        pivot = jnp.sqrt(rest[column])
        values = jnp.where(index >= column, rest / pivot, 0.0)
        factor = factor + values[:, None] * onehot[None, :]
    inner = jnp.zeros_like(gram)
    for line in range(order):
        onehot = (index == line).astype(jnp.float32)
        value = (gram[line, :] - jnp.dot(factor[line, :], inner, precision=highest)) / factor[
            line, line
        ]
        inner = inner + onehot[:, None] * value[None, :]
    solved = jnp.zeros_like(gram)
    for line in range(order - 1, -1, -1):
        onehot = (index == line).astype(jnp.float32)
        value = (inner[line, :] - jnp.dot(factor[:, line], solved, precision=highest)) / factor[
            line, line
        ]
        solved = solved + onehot[:, None] * value[None, :]
    return solved


def per_device(vectors, diag_energy, blocks, block_row, block_col):
    highest = lax.Precision.HIGHEST
    count = vectors.shape[0]
    tiles = blocks[0]
    rows_here = block_row[0]
    cols_here = block_col[0]
    col_whole = lax.all_gather(vectors, "row", axis=1, tiled=True)
    row_whole = lax.all_gather(vectors, "col", axis=1, tiled=True)
    row_blocks = row_whole.shape[1] // BLK
    col_blocks = col_whole.shape[1] // BLK
    col_split = col_whole.reshape(count, col_blocks, BLK)
    row_split = row_whole.reshape(count, row_blocks, BLK)
    picked = col_split[:, cols_here]
    terms = jnp.einsum("bij,kbj->kbi", tiles, picked, precision=highest)
    onehot = (rows_here[:, None] == jnp.arange(row_blocks)[None, :]).astype(jnp.float32)
    part_one = jnp.einsum("kbi,br->kri", terms, onehot, precision=highest).reshape(
        count, row_blocks * BLK
    )
    picked_two = row_split[:, rows_here]
    terms_two = jnp.einsum("bij,kbi->kbj", tiles, picked_two, precision=highest)
    onehot_two = (cols_here[:, None] == jnp.arange(col_blocks)[None, :]).astype(jnp.float32)
    part_two = jnp.einsum("kbj,bq->kqj", terms_two, onehot_two, precision=highest).reshape(
        count, col_blocks * BLK
    )
    own_diag = diag_energy[None, :] * vectors
    metric_local = jnp.dot(
        vectors, vectors.T, precision=highest, preferred_element_type=jnp.float32
    )
    first = lax.psum_scatter(part_one, "col", scatter_dimension=1, tiled=True)
    second = lax.psum_scatter(part_two, "row", scatter_dimension=1, tiled=True)
    image = first + second + own_diag
    quad = jnp.dot(row_whole, part_one.T, precision=highest, preferred_element_type=jnp.float32)
    gram_local = (
        quad
        + quad.T
        + jnp.dot(vectors, own_diag.T, precision=highest, preferred_element_type=jnp.float32)
    )
    gram, metric = lax.psum((gram_local, metric_local), ("row", "col"))
    coef = solve_metric(metric, gram)
    resid = image - jnp.dot(coef.T, vectors, precision=highest, preferred_element_type=jnp.float32)
    return (image, resid)


def solution(mesh):
    return jax.shard_map(
        per_device,
        mesh=mesh,
        in_specs=(
            P(None, ("row", "col")),
            P(("row", "col")),
            P("row", "col", None, None),
            P("row", "col"),
            P("row", "col"),
        ),
        out_specs=(P(None, ("row", "col")), P(None, ("row", "col"))),
        check_vma=False,
    )
```

profile of v0, /device:TPU:0, one launch (start us, length us, event | category | flops | bytes accessed | tf_op | source)
XLA Modules:
  0.0 156.3 jit_solution(4022144908604003280)
XLA Ops:
  7.2 32.7 %all_gather.7 = f32[16,1024]{1,0:T(8,128)S(1)} all-gather(f32[16,128]{1,0:T(8,128)} %param.5), channel_id=1, replica_groups=mesh['row'=4,'col'=8] {'col'}, dimensions={1}, use_global_device_ids=true | all-gather | bytes 73728 | tf_op jit(solution)/shard_map/all_gather | solution.py:44
  41.2 1.4 fusion.7
  43.6 5.2 %all_gather.6 = f32[16,512]{1,0:T(8,128)S(1)} all-gather(f32[16,128]{1,0:T(8,128)S(1)} %copy-done.1), channel_id=1, replica_groups=mesh['row'=4,'col'=8] {'row'}, dimensions={1}, use_global_device_ids=true | all-gather | bytes 40960 | tf_op jit(solution)/shard_map/all_gather | solution.py:43
  49.4 2.5 %fusion.4 = f32[16,24,128]{2,0,1:T(8,128)S(1)} fusion(f32[1,24,128,128]{3,2,1,0:T(8,128)S(1)} %copy-done, f32[24,16,128]{2,1,0:T(8,128)S(1)} %gather_fusion), kind=kOutput, calls=%fused_computation.6 | convolution fusion | flops 75497472 | bytes 1966080 | tf_op jit(solution)/shard_map/bij,kbj->kbi/dot_general | solution.py:50
  53.5 39.6 %all-reduce = (f32[16,16]{1,0:T(8,128)S(1)}, f32[16,16]{1,0:T(8,128)S(1)}) all-reduce(f32[16,16]{1,0:T(8,128)S(1)} %fusion.10, f32[16,16]{1,0:T(8,128)S(1)} %fusion.342), channel_id=1, replica_groups=mesh['row'=4,'col'=8] {'row','col'}, use_global_device_ids=true, to_apply=%region_2.0 | all-reduce | flops 512 | bytes 4096 | tf_op jit(solution)/shard_map/psum | solution.py:74
  121.9 0.9 fusion.60
  122.8 0.9 fusion.61
  124.4 0.8 fusion.63
  125.2 0.8 fusion.64
  126.1 0.8 fusion.65
  126.9 0.8 fusion.66
  128.6 0.8 fusion.68
  129.4 0.8 fusion.69
  130.2 0.8 fusion.70
  131.2 0.8 fusion.71
  132.7 0.9 fusion.73
  133.6 0.9 fusion.74
  134.5 0.8 fusion.75
  135.3 0.8 fusion.76
  136.2 0.8 fusion.77
  136.9 0.9 fusion.78
  137.8 0.8 fusion.79
  138.7 0.8 fusion.80
  139.5 0.8 fusion.81
  140.3 0.9 fusion.82
  142.0 0.8 fusion.84
  142.8 0.8 fusion.85
  143.6 0.8 fusion.86
  145.2 0.9 fusion.88
  146.1 0.9 fusion.89
  147.0 0.8 fusion.90
  148.5 0.9 convolution_subtract_fusion
  (135 shorter events, 27.2 us)
Async XLA Ops:
  7.2 34.0 %copy-start = (f32[1,24,128,128]{3,2,1,0:T(8,128)S(1)}, f32[1,24,128,128]{3,2,1,0:T(8,128)}, u32[]{:S(2)}) copy-start(f32[1,24,128,128]{3,2,1,0:T(8,128)} %param.7) | copy-start | bytes 4718596
  7.2 36.4 %copy-start.1 = (f32[16,128]{1,0:T(8,128)S(1)}, f32[16,128]{1,0:T(8,128)}, u32[]{:S(2)}) copy-start(f32[16,128]{1,0:T(8,128)} %param.5) | copy-start | bytes 24580
  7.2 35.5 %copy-start.4 = (s32[1,24]{1,0:T(1,128)S(1)}, s32[1,24]{1,0:T(1,128)}, u32[]{:S(2)}) copy-start(s32[1,24]{1,0:T(1,128)} %param.9) | copy-start | bytes 292
  7.2 140.6 %reduce-scatter.5.cloned.1.call-start = ((), (), s32[]{:S(2)}) async-start(), calls=%async_computation.3 | async-start | bytes 40960 | tf_op jit(solution)/shard_map/reduce_scatter | solution.py:66
  42.6 9.3 %copy-start.5 = (s32[1,24]{1,0:T(1,128)S(1)}, s32[1,24]{1,0:T(1,128)}, u32[]{:S(2)}) copy-start(s32[1,24]{1,0:T(1,128)} %param.8) | copy-start | bytes 292
  43.5 9.8 %copy-start.3 = (f32[128]{0:T(128)S(1)}, f32[128]{0:T(128)}, u32[]{:S(2)}) copy-start(f32[128]{0:T(128)} %param.6) | copy-start | bytes 1540
  43.5 104.3 %reduce-scatter.3.cloned.1.call-start = ((), (), s32[]{:S(2)}) async-start(), calls=%async_computation.2 | async-start | bytes 73728 | tf_op jit(solution)/shard_map/reduce_scatter | solution.py:65
  148.5 0.9 copy-start.2
Sparse Core Ops, SparseCore 0:
  43.6 20.4 reduce-scatter.4
  67.2 55.0 reduce-scatter.2
where the time goes:
time: 157 us; the launch traced here: 156 us
  blocking collectives  77.5 us (49%)
  matrix products  34.4 us (22%)
  between operations  25 us (16%)
  local copies, waits for them, and re-layouts  15.8 us (10%)
  other arithmetic  3.43 us (2%)
    psum x1, blocking collectives, per_device(): gram, metric = lax.psum((gram_local, metric_local), ('row', 'col'))  39.6 us
    all_gather x1, blocking collectives, per_device(): row_whole = lax.all_gather(vectors, 'col', axis=1, tiled=True)  32.7 us
    dot_general x16, matrix products, solve_metric(): jnp.dot(factor[:, line], solved, precision=highest)  13 us
    dot_general x16, matrix products, solve_metric(): jnp.dot(factor[line, :], inner, precision=highest)  13 us
    slice x15, local copies, waits for them, and re-layouts, solve_metric(): pivot = jnp.sqrt(rest[column])  8.98 us
    all_gather x1, blocking collectives, per_device(): col_whole = lax.all_gather(vectors, 'row', axis=1, tiled=True)  5.19 us
  transfers between devices with their start and end apart: 2, of which 0 were waited for; matrix products, arithmetic and copies ran while one was open for 31% of the time, Pallas kernels for 0%

commit v1 on v0

--- a/solution.py
+++ b/solution.py
@@ -2,6 +2,7 @@
 import jax.numpy as jnp
 from jax import lax
 from jax.sharding import PartitionSpec as P
+from jax.lax import psum
 
 BLK = 128
 
@@ -71,7 +72,12 @@
         + quad.T
         + jnp.dot(vectors, own_diag.T, precision=highest, preferred_element_type=jnp.float32)
     )
-    gram, metric = lax.psum((gram_local, metric_local), ("row", "col"))
+
+    def do_tracks_for(mesh_dim, mine_x, a_name):
+        z_new = psum(psum(mine_x, axis_name=mesh_dim), axis_name=a_name)
+        return z_new
+
+    gram, metric = do_tracks_for("col", (gram_local, metric_local), "row")
     coef = solve_metric(metric, gram)
     resid = image - jnp.dot(coef.T, vectors, precision=highest, preferred_element_type=jnp.float32)
     return (image, resid)

time: 157 us -> 165 us (1.051)
  blocking collectives: 77.5 us -> 85.7 us
    psum x1 -> x2, blocking collectives: 39.6 us -> 47.8 us  [do_tracks_for(): z_new = psum(psum(mine_x, axis_name=mesh_dim), axis_name=a_name)]
  transfers between devices with their start and end apart: 2 -> 2, of which waited for: 0 -> 0; matrix products, arithmetic and copies ran while one was open for 31% -> 30% of each run, Pallas kernels for 0% -> 0%
where the time goes in v1:
time: 165 us; the launch traced here: 164 us
  blocking collectives  85.7 us (52%)
  matrix products  34.4 us (21%)
  between operations  25 us (15%)
  local copies, waits for them, and re-layouts  15.8 us (10%)
  other arithmetic  3.43 us (2%)
    psum x2, blocking collectives, do_tracks_for(): z_new = psum(psum(mine_x, axis_name=mesh_dim), axis_name=a_name)  47.8 us
    all_gather x1, blocking collectives, per_device(): row_whole = lax.all_gather(vectors, 'col', axis=1, tiled=True)  32.7 us
    dot_general x16, matrix products, solve_metric(): jnp.dot(factor[:, line], solved, precision=highest)  13 us
    dot_general x16, matrix products, solve_metric(): jnp.dot(factor[line, :], inner, precision=highest)  13 us
    slice x15, local copies, waits for them, and re-layouts, solve_metric(): pivot = jnp.sqrt(rest[column])  8.98 us
    all_gather x1, blocking collectives, per_device(): col_whole = lax.all_gather(vectors, 'row', axis=1, tiled=True)  5.19 us
  transfers between devices with their start and end apart: 2, of which 0 were waited for; matrix products, arithmetic and copies ran while one was open for 30% of the time, Pallas kernels for 0%

profile of v1, /device:TPU:0, one launch (start us, length us, event | category | flops | bytes accessed | tf_op | source)
XLA Modules:
  0.0 164.4 jit_solution(5783769482973737964)
XLA Ops:
  7.2 32.7 %all_gather.7 = f32[16,1024]{1,0:T(8,128)S(1)} all-gather(f32[16,128]{1,0:T(8,128)} %param.5), channel_id=1, replica_groups=mesh['row'=4,'col'=8] {'col'}, dimensions={1}, use_global_device_ids=true | all-gather | bytes 73728 | tf_op jit(solution)/shard_map/all_gather | solution.py:45
  41.2 1.4 fusion.7
  43.6 5.2 %all_gather.6 = f32[16,512]{1,0:T(8,128)S(1)} all-gather(f32[16,128]{1,0:T(8,128)S(1)} %copy-done.1), channel_id=1, replica_groups=mesh['row'=4,'col'=8] {'row'}, dimensions={1}, use_global_device_ids=true | all-gather | bytes 40960 | tf_op jit(solution)/shard_map/all_gather | solution.py:44
  49.4 2.5 %fusion.4 = f32[16,24,128]{2,0,1:T(8,128)S(1)} fusion(f32[1,24,128,128]{3,2,1,0:T(8,128)S(1)} %copy-done, f32[24,16,128]{2,1,0:T(8,128)S(1)} %gather_fusion), kind=kOutput, calls=%fused_computation.6 | convolution fusion | flops 75497472 | bytes 1966080 | tf_op jit(solution)/shard_map/bij,kbj->kbi/dot_general | solution.py:51
  53.5 37.0 %all-reduce = (f32[16,16]{1,0:T(8,128)S(1)}, f32[16,16]{1,0:T(8,128)S(1)}) all-reduce(f32[16,16]{1,0:T(8,128)S(1)} %fusion.10, f32[16,16]{1,0:T(8,128)S(1)} %fusion.342), channel_id=1, replica_groups=mesh['row'=4,'col'=8] {'col'}, use_global_device_ids=true, to_apply=%region_2.0 | all-reduce | flops 512 | bytes 4096 | tf_op jit(solution)/shard_map/psum | solution.py:77
  90.5 10.8 %all-reduce.1 = (f32[16,16]{1,0:T(8,128)S(1)}, f32[16,16]{1,0:T(8,128)S(1)}) all-reduce(f32[16,16]{1,0:T(8,128)S(1)} %get-tuple-element.34, f32[16,16]{1,0:T(8,128)S(1)} %get-tuple-element.35), channel_id=1, replica_groups=mesh['row'=4,'col'=8] {'row'}, use_global_device_ids=true, to_apply=%region_3.0 | all-reduce | flops 512 | bytes 4096 | tf_op jit(solution)/shard_map/psum | solution.py:77
  130.0 0.9 fusion.60
  130.9 0.9 fusion.61
  132.6 0.8 fusion.63
  133.4 0.8 fusion.64
  134.2 0.8 fusion.65
  135.1 0.8 fusion.66
  136.7 0.8 fusion.68
  137.5 0.8 fusion.69
  138.4 0.8 fusion.70
  139.3 0.8 fusion.71
  140.9 0.9 fusion.73
  141.7 0.9 fusion.74
  142.7 0.8 fusion.75
  143.5 0.8 fusion.76
  145.1 0.9 fusion.78
  146.0 0.8 fusion.79
  146.8 0.8 fusion.80
  147.7 0.8 fusion.81
  148.5 0.9 fusion.82
  150.1 0.8 fusion.84
  151.0 0.8 fusion.85
  151.8 0.8 fusion.86
  153.4 0.9 fusion.88
  154.3 0.9 fusion.89
  155.2 0.8 fusion.90
  156.7 0.9 convolution_subtract_fusion
  (136 shorter events, 28.0 us)
Async XLA Ops:
  7.2 34.0 %copy-start = (f32[1,24,128,128]{3,2,1,0:T(8,128)S(1)}, f32[1,24,128,128]{3,2,1,0:T(8,128)}, u32[]{:S(2)}) copy-start(f32[1,24,128,128]{3,2,1,0:T(8,128)} %param.7) | copy-start | bytes 4718596
  7.2 36.4 %copy-start.1 = (f32[16,128]{1,0:T(8,128)S(1)}, f32[16,128]{1,0:T(8,128)}, u32[]{:S(2)}) copy-start(f32[16,128]{1,0:T(8,128)} %param.5) | copy-start | bytes 24580
  7.2 35.5 %copy-start.4 = (s32[1,24]{1,0:T(1,128)S(1)}, s32[1,24]{1,0:T(1,128)}, u32[]{:S(2)}) copy-start(s32[1,24]{1,0:T(1,128)} %param.9) | copy-start | bytes 292
  7.2 148.8 %reduce-scatter.5.cloned.1.call-start = ((), (), s32[]{:S(2)}) async-start(), calls=%async_computation.3 | async-start | bytes 40960 | tf_op jit(solution)/shard_map/reduce_scatter | solution.py:67
  42.6 9.3 %copy-start.5 = (s32[1,24]{1,0:T(1,128)S(1)}, s32[1,24]{1,0:T(1,128)}, u32[]{:S(2)}) copy-start(s32[1,24]{1,0:T(1,128)} %param.8) | copy-start | bytes 292
  43.5 9.8 %copy-start.3 = (f32[128]{0:T(128)S(1)}, f32[128]{0:T(128)}, u32[]{:S(2)}) copy-start(f32[128]{0:T(128)} %param.6) | copy-start | bytes 1540
  43.5 112.4 %reduce-scatter.3.cloned.1.call-start = ((), (), s32[]{:S(2)}) async-start(), calls=%async_computation.2 | async-start | bytes 73728 | tf_op jit(solution)/shard_map/reduce_scatter | solution.py:66
  156.7 0.9 copy-start.2
Sparse Core Ops, SparseCore 0:
  43.6 20.4 reduce-scatter.4
  67.2 55.0 reduce-scatter.2
